TPU v7x, 32 devices: a whole 2x2x4 slice. The times are simulated.
32 devices in a mesh: chi: 4 (over y, x), dl: 4 (over z), cell: 2 (over core).
Axes of the slice: x: 2, y: 2, z: 4, core: 2. Of those that a mesh axis runs over, the one named last changes fastest.
Arguments:
- left_env: bfloat16 [2, 512, 512, 36], P('cell', None, 'chi'), may hold values from -6 to 6
- up_left: bfloat16 [2, 512, 36, 512], P('cell', 'chi', None, 'dl'), may hold values from -0.109375 to 0.109375
- up_center: bfloat16 [2, 512, 36, 512], P('cell', 'chi', None, 'dl'), may hold values from -0.109375 to 0.109375
- right_env: bfloat16 [2, 512, 36, 512], P('cell', 'dl'), may hold values from -0.046875 to 0.046875
- center: bfloat16 [2, 512, 512], P('cell', None, 'dl'), may hold values from -0.25 to 0.25
- ket_tensor: bfloat16 [2, 6, 6, 6, 6, 2], P('cell'), may hold values from -0.875 to 0.875
Outputs:
- left_env_new: float32 [2, 512, 36, 512], P('cell', 'chi', None, 'dl')
- new_left: float32 [2, 512, 36, 512], P('cell', 'chi', None, 'dl')
All inputs are finite; a program needn't handle non-finite values.
Results may differ from a plain program's by a relative error of at most 0.0066.
The roundings to bfloat16 on the way count: a program that leaves them out, or rounds other values in their place, can miss the bound.
Values may be sent and summed in bfloat16 or wider, within the bound.
A program may use at most 256 MiB of HBM per device.

v0:
```python
import math
import jax
import jax.numpy as jnp
from jax import lax
from jax.experimental.layout import Layout, with_layout_constraint
from jax.sharding import PartitionSpec as P

ITERS = 5
HIGH = lax.Precision.HIGH
F32 = jnp.float32
BF16 = jnp.bfloat16


def from_behind(block, axis, distance):
    devices = range(lax.axis_size(axis))
    route = [((i - distance) % len(devices), i) for i in devices]
    return lax.ppermute(block, axis, route)


def pick(rows, cols, row_of, col_of):
    r = lax.broadcasted_iota(jnp.int32, (rows, cols), 0)
    c = lax.broadcasted_iota(jnp.int32, (rows, cols), 1)
    return (row_of(r) == col_of(c)).astype(BF16)


def double_layer(tensor, pad):
    leg = tensor.shape[0]
    two = leg * leg
    phys = tensor.shape[4]
    big = two * pad

    def outer(first):

        def code(n):
            m, s = (n // pad, n % pad)
            a = m // leg if first else m % leg
            b = s // leg if first else s % leg
            return jnp.where(s < two, a * leg + b, -1)

        return code

    def same(n):
        return n

    total = None
    ket_rows = pick(big, two, outer(True), same)
    bra_rows = pick(big, two, outer(False), same)
    for p in range(phys):
        mat = tensor[:, :, :, :, p].reshape(two, two)
        ket_small = jnp.dot(ket_rows, mat, preferred_element_type=F32).astype(BF16)
        bra_small = jnp.dot(bra_rows, mat, preferred_element_type=F32).astype(BF16)
        ket = lax.dot_general(
            ket_small, ket_rows, (((1,), (1,)), ((), ())), preferred_element_type=F32
        )
        bra = lax.dot_general(
            bra_small, bra_rows, (((1,), (1,)), ((), ())), preferred_element_type=F32
        )
        total = ket * bra if total is None else total + ket * bra
    return total.astype(BF16)


def row_major(block):
    return with_layout_constraint(block, Layout(major_to_minor=tuple(range(block.ndim))))


def site_input(env, stacked):
    summed = jnp.einsum("abm,csa->cmsb", env, stacked, preferred_element_type=F32).astype(BF16)
    summed = row_major(summed)
    columns, two, pad, amount = summed.shape
    return summed.reshape(columns, two * pad, amount)


def site_output(flat, layer, pad):
    out = jnp.einsum("tn,ctb->cnb", layer, flat, preferred_element_type=F32).astype(BF16)
    return out.reshape(out.shape[0], out.shape[1] // pad, pad, out.shape[2])


def spread_rows(block, pad):
    turned = jnp.pad(block.transpose(2, 1, 0), ((0, 0), (0, pad - block.shape[1]), (0, 0)))
    return lax.all_gather(row_major(turned), "chi", axis=2, tiled=True)


def shards(left_env, up_left, up_center, right_env, center, ket_tensor):
    env_local = left_env[0]
    left_iso = up_left[0]
    left_mid = up_center[0]
    env_right = right_env[0]
    bond_mat = center[0]
    site_ket = ket_tensor[0]
    chi_all = env_local.shape[0]
    leg_width = env_local.shape[2]
    pad = -(-leg_width // 8) * 8
    rows = left_iso.shape[0]
    col_count = left_iso.shape[2]
    mid_all = spread_rows(left_mid, pad)
    iso_all = spread_rows(left_iso, pad)
    next_iso = from_behind(left_iso, "cell", -1)
    bra_iso = lax.all_gather(next_iso, "dl", axis=2, tiled=True)
    layer = double_layer(site_ket, pad)
    mixed = jnp.einsum("abm,ax->bmx", env_local, bond_mat, preferred_element_type=F32).astype(BF16)
    bond_term = jnp.einsum("bma,amc->bc", mixed, env_right, preferred_element_type=F32)
    bond_slots = lax.dynamic_update_slice(
        jnp.zeros((chi_all, chi_all), F32), bond_term, (lax.axis_index("chi") * rows, 0)
    )
    mid_all, bond_slots = lax.optimization_barrier((mid_all, bond_slots))
    bond_sum = lax.psum(bond_slots, ("chi", "dl"))
    right_cut = site_output(site_input(env_local, mid_all), layer, pad)
    center_term = jnp.einsum(
        "amdb,amc->bdc", right_cut[:, :, :leg_width], env_right, preferred_element_type=F32
    ).astype(BF16)
    iso_all, center_term, bond_sum = lax.optimization_barrier((iso_all, center_term, bond_sum))
    bond_full = bond_sum.astype(BF16)
    center_part = lax.psum_scatter(center_term, "dl", scatter_dimension=0, tiled=True)
    cross_part = jnp.einsum("bdc,bdy->cy", center_part, center_part, preferred_element_type=F32)

    def env_piece(cut):
        term = jnp.einsum(
            "cmdb,bdk->kmc", cut[:, :, :leg_width], bra_iso, preferred_element_type=F32
        ).astype(BF16)
        return lax.psum_scatter(term, "chi", scatter_dimension=0, tiled=True).astype(F32)

    half = leg_width // 2 * pad
    left_flat = site_input(env_local, iso_all)
    left_early = site_output(left_flat, layer[:, :half], pad)
    left_early, left_flat, cross_part, center_part = lax.optimization_barrier(
        (left_early, left_flat, cross_part, center_part)
    )
    cross = lax.psum(cross_part, ("chi", "dl"))
    center_all = lax.all_gather(center_part, "dl", axis=0, tiled=True)
    left_late = site_output(left_flat, layer[:, half:], pad)
    env_new = jnp.concatenate([env_piece(left_early), env_piece(left_late)], axis=1)
    bond_wide = bond_full.astype(F32)
    gram = jnp.dot(jnp.dot(bond_wide, cross, precision=HIGH), bond_wide.T, precision=HIGH)
    one = jnp.eye(chi_all, dtype=F32)
    norm_sum = jnp.sum(gram * one)
    factor = 0.25 * math.sqrt(chi_all) / jnp.sqrt(norm_sum)
    gram = gram * (factor * factor)
    product = None
    for sweep_index in range(ITERS):
        step = 1.5 * one - 0.5 * gram
        product = step if product is None else jnp.dot(product, step, precision=HIGH)
        if sweep_index < ITERS - 1:
            gram = jnp.dot(jnp.dot(step, gram, precision=HIGH), step, precision=HIGH)
    mine = lax.dynamic_slice_in_dim(product, lax.axis_index("dl") * col_count, col_count, 1)
    weight = lax.dot_general(bond_wide, mine, (((0,), (0,)), ((), ())), precision=HIGH)
    weight = weight * (factor * math.sqrt(chi_all * leg_width))
    new_left = jnp.einsum("bdc,cx->bdx", center_all.astype(F32), weight, precision=HIGH)
    return (env_new[None], new_left[None])


def solution(mesh):
    placed = (
        P("cell", None, "chi", None),
        P("cell", "chi", None, "dl"),
        P("cell", "chi", None, "dl"),
        P("cell", "dl", None, None),
        P("cell", None, "dl"),
        P("cell", None, None, None, None, None),
    )
    return jax.shard_map(
        shards,
        mesh=mesh,
        in_specs=placed,
        out_specs=(P("cell", "chi", None, "dl"), P("cell", "chi", None, "dl")),
        check_vma=False,
    )
```

profile of v0, /device:TPU:0, one launch (start us, length us, event | category | flops | bytes accessed | tf_op | source)
XLA Modules:
  0.0 800.2 jit_solution(4183132327198189968)
XLA Ops:
  7.2 2.2 copy.43
  14.1 7.7 fusion.52
  21.8 11.0 %convolution_multiply_fusion.1 = f32[1440,1440]{1,0:T(8,128)} fusion(f32[1440,1440]{1,0:T(8,128)} %fusion.52, bf16[36,36]{1,0:T(8,128)(2,1)S(1)} %reshape_squeeze.6, s32[1440]{0:T(1024)S(1)} %get-tuple-element.30, s32[1440]{0:T(1024)S(1)} %get-tuple-element.33, s32[1440]{0:T(1024)S(1)} %get-tuple-element.31, s32[1440]{0:T(1024)S(1)} %get-tuple-element.32, ...), kind=kOutput, calls=%fused_computation.13 | convolution fusion | flops 157127040 | bytes 16617312 | tf_op jit(solution)/shard_map/dot_general | solution.py:55
  33.0 7.3 fusion.53
  40.3 12.5 %fusion.7 = bf16[1440,1440]{1,0:T(8,128)(2,1)} fusion(f32[1440,1440]{1,0:T(8,128)} %convolution_multiply_fusion.1, f32[1440,1440]{1,0:T(8,128)} %fusion.53, bf16[36,36]{1,0:T(8,128)(2,1)S(1)} %reshape_squeeze.7, s32[1440]{0:T(1024)S(1)} %get-tuple-element.30, s32[1440]{0:T(1024)S(1)} %get-tuple-element.33, s32[1440]{0:T(1024)S(1)} %get-tuple-element.31, ...), kind=kOutput, calls=%fused_computation.15 | convolution fusion | flops 161274240 | bytes 20764512 | tf_op jit(solution)/shard_map/dot_general | solution.py:55
  52.9 6.5 fusion.49
  59.5 15.4 %all-gather.7.cloned.1.call-done = bf16[128,40,512]{2,1,0:T(8,128)(2,1)} async-done(((bf16[128,40,128]{2,1,0:T(8,128)(2,1)}), bf16[128,40,512]{2,1,0:T(8,128)(2,1)}) %all-gather.7.cloned.1.call-update) | async-done | bytes 5242896 | tf_op jit(solution)/shard_map/all_gather | solution.py:80
  74.8 32.4 %convolution_convert_fusion.2 = bf16[128,40,128,36]{2,1,3,0:T(8,128)(2,1)} fusion(bf16[128,40,512]{2,1,0:T(8,128)(2,1)} %all-gather.7.cloned.1.call-done, bf16[1,512,128,36]{2,1,3,0:T(8,128)(2,1)} %param.6), kind=kOutput, calls=%fused_computation.4 | convolution fusion | flops 24182784000 | bytes 57147392 | tf_op jit(solution)/shard_map/abm,csa->cmsb/dot_general | solution.py:67
  107.2 98.4 %all-reduce.6 = bf16[512,512]{1,0:T(8,128)(2,1)} all-reduce(f32[512,512]{1,0:T(8,128)S(1)} %fusion.49), channel_id=1, replica_groups=mesh['chi'=4,'dl'=4,'cell'=2] {'chi','dl'}, use_global_device_ids=true, to_apply=%region_0.1 | all-reduce | flops 262144 | bytes 1572864 | tf_op jit(solution)/shard_map/psum | solution.py:106
  205.6 81.7 %convolution_convert_fusion = bf16[128,128,1440]{1,2,0:T(8,128)(2,1)} fusion(bf16[128,1440,128]{2,1,0:T(8,128)(2,1)} %bitcast.157, bf16[1440,1440]{1,0:T(8,128)(2,1)} %fusion.7), kind=kOutput, calls=%fused_computation.2 | convolution fusion | flops 67971317760 | bytes 98519040 | tf_op jit(solution)/shard_map/tn,ctb->cnb/dot_general | solution.py:74
  287.3 37.6 %fusion.10 = bf16[128,36,512]{2,0,1:T(8,128)(2,1)} fusion(bf16[1,128,36,512]{3,1,2,0:T(8,128)(2,1)S(1)} %copy-done.7, bf16[128,36,36,128]{3,2,1,0:T(8,128)(2,1)} %bitcast.158), kind=kOutput, calls=%fused_computation.18 | convolution fusion | flops 21745631232 | bytes 51904512 | tf_op jit(solution)/shard_map/amdb,amc->bdc/dot_general | solution.py:108
  326.2 2.8 collective-permute-done
  330.1 32.4 %convolution_convert_fusion.1 = bf16[128,40,128,36]{2,1,3,0:T(8,128)(2,1)} fusion(bf16[128,40,512]{2,1,0:T(8,128)(2,1)} %all-gather.5.cloned.1.call-done, bf16[1,512,128,36]{2,1,3,0:T(8,128)(2,1)} %param.6), kind=kOutput, calls=%fused_computation.3 | convolution fusion | flops 24182784000 | bytes 57147392 | tf_op jit(solution)/shard_map/abm,csa->cmsb/dot_general | solution.py:67
  362.5 45.4 %convolution_convert_fusion.4 = bf16[128,128,720]{1,2,0:T(8,128)(2,1)} fusion(bf16[128,1440,128]{2,1,0:T(8,128)(2,1)} %bitcast.155, bf16[1440,1440]{1,0:T(8,128)(2,1)} %fusion.7), kind=kOutput, calls=%fused_computation.10 | convolution fusion | flops 33985658880 | bytes 72990720 | tf_op jit(solution)/shard_map/tn,ctb->cnb/dot_general | solution.py:74
  408.0 3.6 convolution_bitcast_fusion.1
  411.6 46.5 %convolution_convert_fusion.3 = bf16[128,128,720]{1,2,0:T(8,128)(2,1)} fusion(bf16[128,1440,128]{2,1,0:T(8,128)(2,1)} %bitcast.156, bf16[1440,1440]{1,0:T(8,128)(2,1)} %fusion.7), kind=kOutput, calls=%fused_computation.9 | convolution fusion | flops 33985658880 | bytes 72990720 | tf_op jit(solution)/shard_map/tn,ctb->cnb/dot_general | solution.py:74
  458.2 41.3 %all-gather.9.cloned.1.call-done = bf16[128,36,512]{2,0,1:T(8,128)(2,1)} async-done(((bf16[128,36,128]{2,0,1:T(8,128)(2,1)}), bf16[128,36,512]{2,0,1:T(8,128)(2,1)}) %all-gather.9.cloned.1.call-update) | async-done | bytes 4718608 | tf_op jit(solution)/shard_map/all_gather | solution.py:98
  499.4 15.8 %bitcast_convert_fusion.1 = bf16[128,18,512]{2,0,1:T(8,128)(2,1)S(1)} fusion(bf16[128,36,512]{2,0,1:T(8,128)(2,1)} %all-gather.9.cloned.1.call-done, bf16[128,18,36,128]{3,2,1,0:T(8,128)(2,1)} %bitcast.160), kind=kOutput, calls=%fused_computation.19 | convolution fusion | flops 10872815616 | bytes 28311552 | tf_op jit(solution)/shard_map/cmdb,bdk->kmc/dot_general | solution.py:117
  515.2 2.4 copy.82
  517.7 15.8 %bitcast_convert_fusion.2 = bf16[128,18,512]{2,0,1:T(8,128)(2,1)S(1)} fusion(bf16[128,36,512]{2,0,1:T(8,128)(2,1)} %all-gather.9.cloned.1.call-done, bf16[128,18,40,128]{3,2,1,0:T(8,128)(2,1)} %bitcast.159), kind=kOutput, calls=%fused_computation.20 | convolution fusion | flops 10872815616 | bytes 30670848 | tf_op jit(solution)/shard_map/cmdb,bdk->kmc/dot_general | solution.py:117
  533.5 2.4 copy.80
  536.8 77.7 %all-reduce.5.cloned.1.call-done = f32[512,512]{1,0:T(8,128)} async-done(((f32[512,512]{1,0:T(8,128)}), f32[512,512]{1,0:T(8,128)}) %all-reduce.5.cloned.1.call-update) | async-done | bytes 1048592 | tf_op jit(solution)/shard_map/psum | solution.py:128
  614.5 2.0 fusion.176
  616.5 1.4 select_reduce_fusion
  628.9 1.3 fusion.55
  631.8 22.7 %reduce-scatter.12.cloned.1.call-done = bf16[128,2304]{1,0:T(8,128)(2,1)} async-done(((bf16[512,2304]{1,0:T(8,128)(2,1)}), bf16[128,2304]{1,0:T(8,128)(2,1)}) %reduce-scatter.12.cloned.1.call-update) | async-done | bytes 589840
  654.5 1.4 copy.83
  655.8 39.7 %reduce-scatter.10.cloned.1.call-done = bf16[128,2304]{1,0:T(8,128)(2,1)} async-done(((bf16[512,2304]{1,0:T(8,128)(2,1)}), bf16[128,2304]{1,0:T(8,128)(2,1)}) %reduce-scatter.10.cloned.1.call-update) | async-done | bytes 589840
  695.5 2.1 copy.81
  698.9 2.0 copy.56
  700.8 85.7 %all-gather.11.cloned.1.call-done = bf16[128,36,512]{2,0,1:T(8,128)(2,1)} async-done(((bf16[32,36,512]{2,0,1:T(8,128)(2,1)}), bf16[128,36,512]{2,0,1:T(8,128)(2,1)}) %all-gather.11.cloned.1.call-update) | async-done | bytes 4718608 | tf_op jit(solution)/shard_map/all_gather | solution.py:129
  786.5 6.3 convolution_bitcast_fusion
  (58 shorter events, 21.1 us)
Async XLA Ops:
  7.2 45.8 %copy-start = (bf16[1,512,128]{2,1,0:T(8,128)(2,1)S(1)}, bf16[1,512,128]{2,1,0:T(8,128)(2,1)}, u32[]{:S(2)}) copy-start(bf16[1,512,128]{2,1,0:T(8,128)(2,1)} %param.10) | copy-start | bytes 393220
  7.2 3.6 copy-start.3
  7.2 67.6 %all-gather.7.cloned.1.call-start = ((), (), s32[]{:S(2)}) async-start(), calls=%async_computation.4 | async-start | bytes 6553600 | tf_op jit(solution)/shard_map/all_gather | solution.py:80
  9.5 3.9 copy-start.6
  10.7 314.2 %all-gather.5.cloned.1.call-start = ((), (), s32[]{:S(2)}) async-start(), calls=%async_computation.3 | async-start | bytes 6553600 | tf_op jit(solution)/shard_map/all_gather | solution.py:80
  13.3 394.7 %reduce-scatter.8.cloned.1.call-start = ((), (), s32[]{:S(2)}) async-start(), calls=%async_computation.5 | async-start | bytes 5898240 | tf_op jit(solution)/shard_map/reduce_scatter | solution.py:113
  205.6 81.7 %copy-start.7 = (bf16[1,128,36,512]{3,1,2,0:T(8,128)(2,1)S(1)}, bf16[1,128,36,512]{3,1,2,0:T(8,128)(2,1)}, u32[]{:S(2)}) copy-start(bf16[1,128,36,512]{3,1,2,0:T(8,128)(2,1)} %param.9) | copy-start | bytes 14155780
  324.9 1.3 copy-start.4
  324.9 174.5 %all-gather.9.cloned.1.call-start = ((), (), s32[]{:S(2)}) async-start(), calls=%async_computation.6 | async-start | bytes 5898240 | tf_op jit(solution)/shard_map/all_gather | solution.py:98
  326.2 2.8 collective-permute-start
  329.0 1.0 copy-start.5
  330.1 284.4 %all-reduce.5.cloned.1.call-start = ((), (), s32[]{:S(2)}) async-start(), calls=%async_computation.8 | async-start | bytes 2097152 | tf_op jit(solution)/shard_map/psum | solution.py:128
  458.1 196.4 %reduce-scatter.12.cloned.1.call-start = ((), (), s32[]{:S(2)}) async-start(), calls=%async_computation.10 | async-start | bytes 2949120
  517.6 177.9 %reduce-scatter.10.cloned.1.call-start = ((), (), s32[]{:S(2)}) async-start(), calls=%async_computation.9 | async-start | bytes 2949120
  533.5 81.0 %copy-start.2 = (bf16[512,512]{1,0:T(8,128)(2,1)S(1)}, bf16[512,512]{1,0:T(8,128)(2,1)}, u32[]{:S(2)}) copy-start(bf16[512,512]{1,0:T(8,128)(2,1)} %all-reduce.6) | copy-start | bytes 1572868
  536.0 250.5 %all-gather.11.cloned.1.call-start = ((), (), s32[]{:S(2)}) async-start(), calls=%async_computation.7 | async-start | bytes 5898240 | tf_op jit(solution)/shard_map/all_gather | solution.py:129
  698.9 94.0 %copy-start.1 = (bf16[1,512,128]{2,1,0:T(8,128)(2,1)S(1)}, bf16[1,512,128]{2,1,0:T(8,128)(2,1)}, u32[]{:S(2)}) copy-start(bf16[1,512,128]{2,1,0:T(8,128)(2,1)} %param.10) | copy-start | bytes 393220
Sparse Core Ops, SparseCore 0:
  10.8 63.9 all-gather.6
  77.2 69.7 all-gather.4
  325.1 82.6 reduce-scatter.7
  409.7 89.6 all-gather.8
  504.6 109.8 all-reduce.4
  618.0 36.4 reduce-scatter.11
  658.1 37.3 reduce-scatter.9
  697.1 89.3 all-gather.10
where the time goes:
time: 810 us; the launch traced here: 800 us
  matrix products  379 us (47%)
  waiting for transfers between devices  286 us (35%)
  blocking collectives  98.4 us (12%)
  local copies, waits for them, and re-layouts  19.4 us (2%)
  between operations  15.5 us (2%)
    dot_general x3, matrix products, site_output(): jnp.einsum('tn,ctb->cnb', layer, flat, preferred_element_type=F32)  174 us
    psum x1, blocking collectives, shards(): bond_sum = lax.psum(bond_slots, ('chi', 'dl'))  98.4 us
    all_gather x1, waiting for transfers between devices, shards(): center_all = lax.all_gather(center_part, 'dl', axis=0, tiled=True)  85.7 us
    psum x1, waiting for transfers between devices, shards(): cross = lax.psum(cross_part, ('chi', 'dl'))  77.7 us
    dot_general x2, matrix products, site_input(): jnp.einsum('abm,csa->cmsb', env, stacked, preferred_element_type=F32)  64.8 us
    unnamed x10, waiting for transfers between devices  63 us
    all_gather x1, waiting for transfers between devices, shards(): bra_iso = lax.all_gather(next_iso, 'dl', axis=2, tiled=True)  41.3 us
    dot_general x1, matrix products, shards(): jnp.einsum('amdb,amc->bdc', right_cut[:, :, :leg_width], env_right, prefe...  37.6 us
  transfers between devices with their start and end apart: 9, of which 7 were waited for; matrix products, arithmetic and copies ran while one was open for 48% of the time, Pallas kernels for 0%

commit v1 on v0

--- a/solution.py
+++ b/solution.py
@@ -9,6 +9,16 @@
 HIGH = lax.Precision.HIGH
 F32 = jnp.float32
 BF16 = jnp.bfloat16
+
+
+def ring_gather(x, axis, dim):
+    ways, here, turn = (lax.axis_size(axis), lax.axis_index(axis), x.shape[dim])
+    lengths = [n * ways if d == dim else n for d, n in enumerate(x.shape)]
+    full = lax.dynamic_update_slice_in_dim(jnp.zeros(lengths, x.dtype), x, here * turn, axis=dim)
+    for far in range(1, ways):
+        x = lax.ppermute(x, axis, [(d, (d + 1) % ways) for d in range(ways)])
+        full = lax.dynamic_update_slice_in_dim(full, x, (here - far) % ways * turn, axis=dim)
+    return full
 
 
 def from_behind(block, axis, distance):
@@ -126,7 +136,7 @@
         (left_early, left_flat, cross_part, center_part)
     )
     cross = lax.psum(cross_part, ("chi", "dl"))
-    center_all = lax.all_gather(center_part, "dl", axis=0, tiled=True)
+    center_all = ring_gather(center_part, "dl", 0)
     left_late = site_output(left_flat, layer[:, half:], pad)
     env_new = jnp.concatenate([env_piece(left_early), env_piece(left_late)], axis=1)
     bond_wide = bond_full.astype(F32)

time: 810 us -> 738 us (0.911)
  waiting for transfers between devices: 286 us -> 197 us
  local copies, waits for them, and re-layouts: 19.4 us -> 32.1 us
    all_gather x1 -> x0, waiting for transfers between devices: 85.7 us -> none  [shards(): center_all = lax.all_gather(center_part, 'dl', axis=0, tiled=True)]
    unnamed x10 -> x9, waiting for transfers between devices: 63 us -> 4.05 us
    ppermute x0 -> x3, waiting for transfers between devices: none -> 41.3 us  [ring_gather(): x = lax.ppermute(x, axis, [(d, (d + 1) % ways) for d in range(ways)])]
    all_gather x1, waiting for transfers between devices: 41.3 us -> 58.2 us  [shards(): bra_iso = lax.all_gather(next_iso, 'dl', axis=2, tiled=True)]
    dynamic_update_slice x0 -> x4, local copies, waits for them, and re-layouts: none -> 9.86 us  [the longest x3 7.36 us: ring_gather(): lax.dynamic_update_slice_in_dim(full, x, (here - far) % ways * turn, axis...]
  transfers between devices with their start and end apart: 9 -> 11, of which waited for: 7 -> 7; matrix products, arithmetic and copies ran while one was open for 48% -> 56% of each run, Pallas kernels for 0% -> 0%
where the time goes in v1:
time: 738 us; the launch traced here: 728 us
  matrix products  382 us (52%)
  waiting for transfers between devices  197 us (27%)
  blocking collectives  98.4 us (13%)
  local copies, waits for them, and re-layouts  32.1 us (4%)
  between operations  15.3 us (2%)
    dot_general x3, matrix products, site_output(): jnp.einsum('tn,ctb->cnb', layer, flat, preferred_element_type=F32)  174 us
    psum x1, blocking collectives, shards(): bond_sum = lax.psum(bond_slots, ('chi', 'dl'))  98.4 us
    psum x1, waiting for transfers between devices, shards(): cross = lax.psum(cross_part, ('chi', 'dl'))  75.1 us
    dot_general x2, matrix products, site_input(): jnp.einsum('abm,csa->cmsb', env, stacked, preferred_element_type=F32)  64.8 us
    all_gather x1, waiting for transfers between devices, shards(): bra_iso = lax.all_gather(next_iso, 'dl', axis=2, tiled=True)  58.2 us
    ppermute x3, waiting for transfers between devices, ring_gather(): x = lax.ppermute(x, axis, [(d, (d + 1) % ways) for d in range(ways)])  41.3 us
    dot_general x1, matrix products, shards(): jnp.einsum('amdb,amc->bdc', right_cut[:, :, :leg_width], env_right, prefe...  37.8 us
    dot_general x2, matrix products, env_piece(): jnp.einsum('cmdb,bdk->kmc', cut[:, :, :leg_width], bra_iso, preferred_ele...  32.1 us
  transfers between devices with their start and end apart: 11, of which 7 were waited for; matrix products, arithmetic and copies ran while one was open for 56% of the time, Pallas kernels for 0%

profile of v1, /device:TPU:0, one launch (start us, length us, event | category | flops | bytes accessed | tf_op | source)
XLA Modules:
  0.0 728.3 jit_solution(12330461004539416645)
XLA Ops:
  7.2 2.2 copy.43
  14.1 7.7 %fusion.52 = f32[1440,1440]{1,0:T(8,128)} fusion(bf16[36,36]{1,0:T(8,128)(2,1)S(1)} %reshape_squeeze.6, s32[1440]{0:T(1024)S(1)} %get-tuple-element.30, s32[1440]{0:T(1024)S(1)} %get-tuple-element.33, s32[1440]{0:T(1024)S(1)} %get-tuple-element.31, s32[1440]{0:T(1024)S(1)} %get-tuple-element.32, pred[1440]{0:T(1024)(128)(4,1)S(1)} %get-tuple-element.34, ...), kind=kOutput, calls=%fused_computation.67 | convolution fusion | flops 155468160 | bytes 8322912 | tf_op jit(solution)/shard_map/dot_general | solution.py:62
  21.8 11.0 %convolution_multiply_fusion.1 = f32[1440,1440]{1,0:T(8,128)} fusion(f32[1440,1440]{1,0:T(8,128)} %fusion.52, bf16[36,36]{1,0:T(8,128)(2,1)S(1)} %reshape_squeeze.6, s32[1440]{0:T(1024)S(1)} %get-tuple-element.30, s32[1440]{0:T(1024)S(1)} %get-tuple-element.33, s32[1440]{0:T(1024)S(1)} %get-tuple-element.31, s32[1440]{0:T(1024)S(1)} %get-tuple-element.32, ...), kind=kOutput, calls=%fused_computation.13 | convolution fusion | flops 157127040 | bytes 16617312 | tf_op jit(solution)/shard_map/dot_general | solution.py:65
  33.0 7.3 %fusion.53 = f32[1440,1440]{1,0:T(8,128)} fusion(bf16[36,36]{1,0:T(8,128)(2,1)S(1)} %reshape_squeeze.7, s32[1440]{0:T(1024)S(1)} %get-tuple-element.30, s32[1440]{0:T(1024)S(1)} %get-tuple-element.33, s32[1440]{0:T(1024)S(1)} %get-tuple-element.31, s32[1440]{0:T(1024)S(1)} %get-tuple-element.32, pred[1440]{0:T(1024)(128)(4,1)S(1)} %get-tuple-element.34, ...), kind=kOutput, calls=%fused_computation.68 | convolution fusion | flops 155468160 | bytes 8322912 | tf_op jit(solution)/shard_map/dot_general | solution.py:62
  40.3 12.4 %fusion.7 = bf16[1440,1440]{1,0:T(8,128)(2,1)} fusion(f32[1440,1440]{1,0:T(8,128)} %convolution_multiply_fusion.1, f32[1440,1440]{1,0:T(8,128)} %fusion.53, bf16[36,36]{1,0:T(8,128)(2,1)S(1)} %reshape_squeeze.7, s32[1440]{0:T(1024)S(1)} %get-tuple-element.30, s32[1440]{0:T(1024)S(1)} %get-tuple-element.33, s32[1440]{0:T(1024)S(1)} %get-tuple-element.31, ...), kind=kOutput, calls=%fused_computation.15 | convolution fusion | flops 161274240 | bytes 20764512 | tf_op jit(solution)/shard_map/dot_general | solution.py:65
  52.9 6.5 fusion.49
  59.4 15.4 %all-gather.6.cloned.1.call-done = bf16[128,40,512]{2,1,0:T(8,128)(2,1)} async-done(((bf16[128,40,128]{2,1,0:T(8,128)(2,1)}), bf16[128,40,512]{2,1,0:T(8,128)(2,1)}) %all-gather.6.cloned.1.call-update) | async-done | bytes 5242896 | tf_op jit(solution)/shard_map/all_gather | solution.py:90
  74.8 32.4 %convolution_convert_fusion.2 = bf16[128,40,128,36]{2,1,3,0:T(8,128)(2,1)} fusion(bf16[128,40,512]{2,1,0:T(8,128)(2,1)} %all-gather.6.cloned.1.call-done, bf16[1,512,128,36]{2,1,3,0:T(8,128)(2,1)} %param.6), kind=kOutput, calls=%fused_computation.4 | convolution fusion | flops 24182784000 | bytes 57147392 | tf_op jit(solution)/shard_map/abm,csa->cmsb/dot_general | solution.py:77
  107.3 98.4 %all-reduce.6 = bf16[512,512]{1,0:T(8,128)(2,1)} all-reduce(f32[512,512]{1,0:T(8,128)S(1)} %fusion.49), channel_id=1, replica_groups=mesh['chi'=4,'dl'=4,'cell'=2] {'chi','dl'}, use_global_device_ids=true, to_apply=%region_0.1 | all-reduce | flops 262144 | bytes 1572864 | tf_op jit(solution)/shard_map/psum | solution.py:116
  205.7 81.7 %convolution_convert_fusion = bf16[128,128,1440]{1,2,0:T(8,128)(2,1)} fusion(bf16[128,1440,128]{2,1,0:T(8,128)(2,1)} %bitcast.157, bf16[1440,1440]{1,0:T(8,128)(2,1)} %fusion.7), kind=kOutput, calls=%fused_computation.2 | convolution fusion | flops 67971317760 | bytes 98519040 | tf_op jit(solution)/shard_map/tn,ctb->cnb/dot_general | solution.py:84
  287.4 37.8 %fusion.10 = bf16[128,36,512]{2,0,1:T(8,128)(2,1)} fusion(bf16[1,128,36,512]{3,1,2,0:T(8,128)(2,1)S(1)} %copy-done.7, bf16[128,36,36,128]{3,2,1,0:T(8,128)(2,1)} %bitcast.158), kind=kOutput, calls=%fused_computation.18 | convolution fusion | flops 21745631232 | bytes 51904512 | tf_op jit(solution)/shard_map/amdb,amc->bdc/dot_general | solution.py:118
  326.5 2.8 collective-permute-done
  330.4 32.4 %convolution_convert_fusion.1 = bf16[128,40,128,36]{2,1,3,0:T(8,128)(2,1)} fusion(bf16[128,40,512]{2,1,0:T(8,128)(2,1)} %all-gather.4.cloned.1.call-done, bf16[1,512,128,36]{2,1,3,0:T(8,128)(2,1)} %param.6), kind=kOutput, calls=%fused_computation.3 | convolution fusion | flops 24182784000 | bytes 57147392 | tf_op jit(solution)/shard_map/abm,csa->cmsb/dot_general | solution.py:77
  362.8 45.2 %convolution_convert_fusion.4 = bf16[128,128,720]{1,2,0:T(8,128)(2,1)} fusion(bf16[128,1440,128]{2,1,0:T(8,128)(2,1)} %bitcast.155, bf16[1440,1440]{1,0:T(8,128)(2,1)} %fusion.7), kind=kOutput, calls=%fused_computation.10 | convolution fusion | flops 33985658880 | bytes 72990720 | tf_op jit(solution)/shard_map/tn,ctb->cnb/dot_general | solution.py:84
  408.1 3.6 convolution_bitcast_fusion.1
  412.7 47.0 %convolution_convert_fusion.3 = bf16[128,128,720]{1,2,0:T(8,128)(2,1)} fusion(bf16[128,1440,128]{2,1,0:T(8,128)(2,1)} %bitcast.156, bf16[1440,1440]{1,0:T(8,128)(2,1)} %fusion.7), kind=kOutput, calls=%fused_computation.9 | convolution fusion | flops 33985658880 | bytes 72990720 | tf_op jit(solution)/shard_map/tn,ctb->cnb/dot_general | solution.py:84
  459.7 58.2 %all-gather.8.cloned.1.call-done = bf16[128,36,512]{2,0,1:T(8,128)(2,1)} async-done(((bf16[128,36,128]{2,0,1:T(8,128)(2,1)}), bf16[128,36,512]{2,0,1:T(8,128)(2,1)}) %all-gather.8.cloned.1.call-update) | async-done | bytes 4718608 | tf_op jit(solution)/shard_map/all_gather | solution.py:108
  517.9 15.8 %bitcast_convert_fusion.1 = bf16[128,18,512]{2,0,1:T(8,128)(2,1)S(1)} fusion(bf16[128,36,512]{2,0,1:T(8,128)(2,1)} %all-gather.8.cloned.1.call-done, bf16[128,18,36,128]{3,2,1,0:T(8,128)(2,1)} %bitcast.160), kind=kOutput, calls=%fused_computation.19 | convolution fusion | flops 10872815616 | bytes 28311552 | tf_op jit(solution)/shard_map/cmdb,bdk->kmc/dot_general | solution.py:127
  533.7 2.4 copy.82
  536.2 16.3 %bitcast_convert_fusion.2 = bf16[128,18,512]{2,0,1:T(8,128)(2,1)S(1)} fusion(bf16[128,36,512]{2,0,1:T(8,128)(2,1)} %all-gather.8.cloned.1.call-done, bf16[128,18,40,128]{3,2,1,0:T(8,128)(2,1)} %bitcast.159), kind=kOutput, calls=%fused_computation.20 | convolution fusion | flops 10872815616 | bytes 30670848 | tf_op jit(solution)/shard_map/cmdb,bdk->kmc/dot_general | solution.py:127
  552.5 2.6 copy.80
  555.1 2.7 broadcast_in_dim.21
  557.8 2.5 constant_dynamic-update-slice_fusion.3
  560.3 75.1 %all-reduce.5.cloned.1.call-done = f32[512,512]{1,0:T(8,128)} async-done(((f32[512,512]{1,0:T(8,128)}), f32[512,512]{1,0:T(8,128)}) %all-reduce.5.cloned.1.call-update) | async-done | bytes 1048592 | tf_op jit(solution)/shard_map/psum | solution.py:138
  650.6 23.2 %collective-permute-done.2 = bf16[32,36,512]{2,0,1:T(8,128)(2,1)} collective-permute-done((bf16[32,36,512]{2,0,1:T(8,128)(2,1)}, bf16[32,36,512]{2,0,1:T(8,128)(2,1)}, u32[]{:S(2)}, u32[]{:S(2)}) %collective-permute-start.2) | collective-permute-done | bytes 1179680 | tf_op jit(solution)/shard_map/ppermute | solution.py:19
  675.9 2.2 fusion.175
  678.6 2.5 constant_dynamic-update-slice_fusion.2
  681.1 2.4 constant_dynamic-update-slice_fusion.1
  683.6 18.1 %collective-permute-done.3 = bf16[32,36,512]{2,0,1:T(8,128)(2,1)} collective-permute-done((bf16[32,36,512]{2,0,1:T(8,128)(2,1)}, bf16[32,36,512]{2,0,1:T(8,128)(2,1)}, u32[]{:S(2)}, u32[]{:S(2)}) %collective-permute-start.3) | collective-permute-done | bytes 1179680 | tf_op jit(solution)/shard_map/ppermute | solution.py:19
  701.7 2.4 constant_dynamic-update-slice_fusion
  704.1 6.5 convolution_bitcast_fusion
  712.0 3.9 reduce-scatter.10.cloned.1.call-done
  (66 shorter events, 32.0 us)
Async XLA Ops:
  7.2 45.7 %copy-start = (bf16[1,512,128]{2,1,0:T(8,128)(2,1)S(1)}, bf16[1,512,128]{2,1,0:T(8,128)(2,1)}, u32[]{:S(2)}) copy-start(bf16[1,512,128]{2,1,0:T(8,128)(2,1)} %param.10) | copy-start | bytes 393220
  7.2 3.6 copy-start.3
  7.2 67.6 %all-gather.6.cloned.1.call-start = ((), (), s32[]{:S(2)}) async-start(), calls=%async_computation.4 | async-start | bytes 6553600 | tf_op jit(solution)/shard_map/all_gather | solution.py:90
  9.5 3.9 copy-start.6
  10.7 314.5 %all-gather.4.cloned.1.call-start = ((), (), s32[]{:S(2)}) async-start(), calls=%async_computation.3 | async-start | bytes 6553600 | tf_op jit(solution)/shard_map/all_gather | solution.py:90
  13.3 394.8 %reduce-scatter.8.cloned.1.call-start = ((), (), s32[]{:S(2)}) async-start(), calls=%async_computation.5 | async-start | bytes 5898240 | tf_op jit(solution)/shard_map/reduce_scatter | solution.py:123
  205.7 81.7 %copy-start.7 = (bf16[1,128,36,512]{3,1,2,0:T(8,128)(2,1)S(1)}, bf16[1,128,36,512]{3,1,2,0:T(8,128)(2,1)}, u32[]{:S(2)}) copy-start(bf16[1,128,36,512]{3,1,2,0:T(8,128)(2,1)} %param.9) | copy-start | bytes 14155780
  325.2 1.3 copy-start.4
  325.2 192.7 %all-gather.8.cloned.1.call-start = ((), (), s32[]{:S(2)}) async-start(), calls=%async_computation.6 | async-start | bytes 5898240 | tf_op jit(solution)/shard_map/all_gather | solution.py:108
  326.5 2.8 collective-permute-start
  329.3 1.0 copy-start.5
  330.4 305.1 %all-reduce.5.cloned.1.call-start = ((), (), s32[]{:S(2)}) async-start(), calls=%async_computation.7 | async-start | bytes 2097152 | tf_op jit(solution)/shard_map/psum | solution.py:138
  411.7 233.1 %collective-permute-start.1 = (bf16[32,36,512]{2,0,1:T(8,128)(2,1)}, bf16[32,36,512]{2,0,1:T(8,128)(2,1)}, u32[]{:S(2)}, u32[]{:S(2)}) collective-permute-start(bf16[32,36,512]{2,0,1:T(8,128)(2,1)} %reduce-scatter.8.cloned.1.call-done), channel_id=1, source_target_pairs={{0,2},{2,4},{4,6},{6,0},{1,3},{3,5},{5,7},{7,1},{8,10},{10,12},{12... | collective-permute-start | bytes 3538952 | tf_op jit(solution)/shard_map/ppermute | solution.py:19
  459.7 250.9 %reduce-scatter.12.cloned.1.call-start = ((), (), s32[]{:S(2)}) async-start(), calls=%async_computation.9 | async-start | bytes 2949120
  536.2 179.8 %reduce-scatter.10.cloned.1.call-start = ((), (), s32[]{:S(2)}) async-start(), calls=%async_computation.8 | async-start | bytes 2949120
  555.1 80.3 %copy-start.2 = (bf16[512,512]{1,0:T(8,128)(2,1)S(1)}, bf16[512,512]{1,0:T(8,128)(2,1)}, u32[]{:S(2)}) copy-start(bf16[512,512]{1,0:T(8,128)(2,1)} %all-reduce.6) | copy-start | bytes 1572868
  644.7 29.0 %collective-permute-start.2 = (bf16[32,36,512]{2,0,1:T(8,128)(2,1)}, bf16[32,36,512]{2,0,1:T(8,128)(2,1)}, u32[]{:S(2)}, u32[]{:S(2)}) collective-permute-start(bf16[32,36,512]{2,0,1:T(8,128)(2,1)} %collective-permute-done.1), channel_id=1, source_target_pairs={{0,2},{2,4},{4,6},{6,0},{1,3},{3,5},{5,7},{7,1},{8,10},{10,12},{12... | collective-permute-start | bytes 3538952 | tf_op jit(solution)/shard_map/ppermute | solution.py:19
  673.8 27.9 %collective-permute-start.3 = (bf16[32,36,512]{2,0,1:T(8,128)(2,1)}, bf16[32,36,512]{2,0,1:T(8,128)(2,1)}, u32[]{:S(2)}, u32[]{:S(2)}) collective-permute-start(bf16[32,36,512]{2,0,1:T(8,128)(2,1)} %collective-permute-done.2), channel_id=1, source_target_pairs={{0,2},{2,4},{4,6},{6,0},{1,3},{3,5},{5,7},{7,1},{8,10},{10,12},{12... | collective-permute-start | bytes 3538952 | tf_op jit(solution)/shard_map/ppermute | solution.py:19
  710.6 10.6 %copy-start.1 = (bf16[1,512,128]{2,1,0:T(8,128)(2,1)S(1)}, bf16[1,512,128]{2,1,0:T(8,128)(2,1)}, u32[]{:S(2)}) copy-start(bf16[1,512,128]{2,1,0:T(8,128)(2,1)} %param.10) | copy-start | bytes 393220
Sparse Core Ops, SparseCore 0:
  10.8 63.9 all-gather.5
  77.2 69.7 all-gather.3
  325.4 82.1 reduce-scatter.7
  409.6 108.2 all-gather.7
  523.1 112.3 all-reduce.4
  639.0 36.4 reduce-scatter.11
  678.5 37.3 reduce-scatter.9
